TPU v7x, 32 devices: a whole 2x2x4 slice. The times are simulated.
32 devices in a mesh: member: 2 (over x), gx: 16 (over z, y, core).
Axes of the slice: x: 2, y: 2, z: 4, core: 2. Of those that a mesh axis runs over, the one named last changes fastest.
Arguments:
- electric: float32 [3, 64, 256, 128], P(None, 'gx'), may hold values from -6 to 6
- magnetic: float32 [3, 64, 256, 128], P(None, 'gx'), may hold values from -6 to 6
- material: int32 [128, 256, 128], P(('member', 'gx')), parts along dimension 0, may hold values from 0 to 3, as said below
- permittivity: float32 [4], replicated, may hold values from 1 to 4
- pole_frequency: float32 [2], replicated, may hold values from 0.3 to 1.2
- pole_damping: float32 [2], replicated, may hold values from 0.05 to 1
- pole_strength: float32 [2], replicated, may hold values from 0.3 to 2
- frequencies: float32 [8], replicated, may hold values from 0.2 to 2
- plane_depth: int32 [4], replicated, may hold values from 1 to 126
- mode_fields: float32 [4, 4, 64, 256], P(None, None, 'gx'), may hold values from -40 to 40
Outputs:
- electric_final: float32 [3, 128, 256, 128], P(None, ('member', 'gx')), parts along dimension 1
- magnetic_final: float32 [3, 128, 256, 128], P(None, ('member', 'gx')), parts along dimension 1
- monitors: float32 [2, 4, 8, 4, 128, 256], P(None, None, None, None, ('member', 'gx')), parts along dimension 4
- intersection: float32 [4, 4, 8], P('member'), parts along dimension 0
There are 2 independent parts, one for each index of `member`. A program takes and returns all parts, laid end to end along the dimension named above; an argument that names none is the same for every part. Nothing has to cross between parts.
Inputs may be any that keep to these rules, and one draw needn't show every extreme that they name: Each 16-layer thickness profile stacks layers along the first dimension, each of one material, with a lateral lattice of material 0 cells in some layers; materials 2 and above are dispersive.
All inputs are finite; a program needn't handle non-finite values.
Results may differ from a plain program's by a relative error of at most 0.0003.
Values sent between devices are 32-bit elements; how exact they have to be, the bound alone decides.
A program may use at most 64 MiB of HBM per device.

v0:
```python
import math
import jax
import jax.numpy as jnp
from jax import lax
from jax.sharding import PartitionSpec as P

STEPS = 6
DT = 0.5


def shifted(value, axis, steps):
    count = lax.axis_size(axis)
    first, last = (max(0, -steps), min(count, count - steps))
    return lax.ppermute(value, axis, [(source, source + steps) for source in range(first, last)])


def zero_rim(field, direction):
    return jnp.zeros_like(lax.slice_in_dim(field, 0, 1, axis=direction))


def diff_ahead(field, direction, beyond):
    remainder = lax.slice_in_dim(field, 1, field.shape[direction], axis=direction)
    return jnp.concatenate([remainder, beyond], axis=direction) - field


def diff_behind(field, direction, preceding):
    remainder = lax.slice_in_dim(field, 0, field.shape[direction] - 1, axis=direction)
    return field - jnp.concatenate([preceding, remainder], axis=direction)


def ahead_open(field, direction):
    return diff_ahead(field, direction, zero_rim(field, direction))


def behind_open(field, direction):
    return diff_behind(field, direction, zero_rim(field, direction))


def curl_e(e_field, upper):
    first = ahead_open(e_field[2], 1) - ahead_open(e_field[1], 2)
    second = ahead_open(e_field[0], 2) - diff_ahead(e_field[2], 0, upper[1])
    third = diff_ahead(e_field[1], 0, upper[0]) - ahead_open(e_field[0], 1)
    return jnp.stack([first, second, third])


def curl_h(h_field, lower):
    first = behind_open(h_field[2], 1) - behind_open(h_field[1], 2)
    second = behind_open(h_field[0], 2) - diff_behind(h_field[2], 0, lower[1])
    third = diff_behind(h_field[1], 0, lower[0]) - behind_open(h_field[0], 1)
    return jnp.stack([first, second, third])


def coefficients(material, permittivity, pole_frequency, pole_damping, pole_strength):
    eps_cell = jnp.zeros(material.shape, jnp.float32)
    for kind_index in range(permittivity.shape[0]):
        eps_cell = eps_cell + jnp.where(material == kind_index, permittivity[kind_index], 0.0)
    damping = jnp.zeros(material.shape, jnp.float32)
    square = jnp.zeros(material.shape, jnp.float32)
    driving = jnp.zeros(material.shape, jnp.float32)
    offset = permittivity.shape[0] - pole_frequency.shape[0]
    for pole_index in range(pole_frequency.shape[0]):
        chosen = material == pole_index + offset
        freq_sq = pole_frequency[pole_index] * pole_frequency[pole_index]
        damping = damping + jnp.where(chosen, pole_damping[pole_index], 0.0)
        square = square + jnp.where(chosen, freq_sq, 0.0)
        driving = driving + jnp.where(chosen, pole_strength[pole_index] * freq_sq, 0.0)
    divisor = 1.0 + 0.5 * DT * damping
    retain = (1.0 - 0.5 * DT * damping) / divisor
    pulling = DT * driving / divisor
    spring = DT * square / divisor
    step_e = DT / eps_cell
    return (retain, pulling, spring, step_e)


def record(monitors, e_field, h_field, select, frequencies, step):
    plane_e = jnp.einsum("cxyz,zm->cmxy", e_field[:2], select, precision=lax.Precision.HIGHEST)
    plane_h = jnp.einsum("cxyz,zm->cmxy", h_field[:2], select, precision=lax.Precision.HIGHEST)
    planes = jnp.concatenate([plane_e, plane_h], axis=0)
    phase_e = (step + 1.0) * DT * frequencies
    phase_h = (step + 0.5) * DT * frequencies
    cosines = jnp.stack([jnp.cos(phase_e), jnp.cos(phase_e), jnp.cos(phase_h), jnp.cos(phase_h)])
    sine_part = -jnp.stack([jnp.sin(phase_e), jnp.sin(phase_e), jnp.sin(phase_h), jnp.sin(phase_h)])
    rotation = jnp.stack([cosines, sine_part])
    return monitors + rotation[:, :, :, None, None, None] * planes[None, :, None, :, :, :]


def project(monitors, mode_fields, scale):
    pairing = jnp.stack([mode_fields[3], -mode_fields[2], -mode_fields[1], mode_fields[0]])
    return scale * jnp.einsum(
        "rcfmxy,cmxy->rmf", monitors, pairing, precision=lax.Precision.HIGHEST
    )


def pole_update(current, polarized, e_field, curl_field, retain, pulling, spring, step_e):
    current = retain * current + pulling * e_field - spring * polarized
    polarized = polarized + DT * current
    e_field = e_field + step_e * (curl_field - current)
    return (current, polarized, e_field)


def on_device(
    electric,
    magnetic,
    material,
    permittivity,
    pole_frequency,
    pole_damping,
    pole_strength,
    frequencies,
    plane_depth,
    mode_fields,
):
    retain, pulling, spring, step_e = coefficients(
        material, permittivity, pole_frequency, pole_damping, pole_strength
    )
    slab_cells = electric.shape[1]
    width_y = electric.shape[2]
    depth_z = electric.shape[3]
    select = (jnp.arange(depth_z)[:, None] == plane_depth[None, :]).astype(jnp.float32)
    current = jnp.zeros_like(electric)
    polarized = jnp.zeros_like(electric)
    monitors = jnp.zeros(
        (2, 4, frequencies.shape[0], plane_depth.shape[0], slab_cells, width_y), jnp.float32
    )
    for step in range(STEPS):
        upper = shifted(electric[1:3, :1], "gx", -1)
        magnetic = magnetic - DT * curl_e(electric, upper)
        lower = shifted(magnetic[1:3, -1:], "gx", 1)
        curl_field = curl_h(magnetic, lower)
        current, polarized, electric = pole_update(
            current, polarized, electric, curl_field, retain, pulling, spring, step_e
        )
        monitors = record(monitors, electric, magnetic, select, frequencies, step)
    scale = 1.0 / math.sqrt(4.0 * slab_cells * lax.axis_size("gx") * width_y)
    partial_value = project(monitors, mode_fields, scale)
    intersection = lax.psum(partial_value, "gx")
    return (electric, magnetic, monitors, intersection)


def solution(mesh):
    in_specs = (
        P(None, "gx", None, None),
        P(None, "gx", None, None),
        P(("member", "gx"), None, None),
        P(),
        P(),
        P(),
        P(),
        P(),
        P(),
        P(None, None, "gx", None),
    )
    out_specs = (
        P(None, ("member", "gx"), None, None),
        P(None, ("member", "gx"), None, None),
        P(None, None, None, None, ("member", "gx"), None),
        P("member", None, None),
    )
    return jax.shard_map(
        on_device, mesh=mesh, in_specs=in_specs, out_specs=out_specs, check_vma=False
    )
```

profile of v0, /device:TPU:0, one launch (start us, length us, event | category | flops | bytes accessed | tf_op | source)
XLA Modules:
  0.0 158.4 jit_solution(6075497116907819001)
XLA Ops:
  0.6 1.0 slice.656
  1.7 1.4 collective-permute-start
  3.1 1.5 slice_bitcast_fusion.35
  4.6 0.6 fusion.102
  7.8 0.6 fusion.103
  8.4 0.6 fusion.101
  9.0 0.7 fusion.100
  11.3 1.6 subtract_divide_fusion
  13.0 4.4 %broadcast_multiply_fusion.2 = (f32[4,256,128]{2,1,0:T(8,128)S(1)}, f32[4,256,128]{2,1,0:T(8,128)S(1)}, f32[4,256,128]{2,1,0:T(8,128)S(1)}, f32[4,256,128]{2,1,0:T(8,128)S(1)}, f32[4,256,128]{2,1,0:T(8,128)S(1)}) fusion(pred[4,256,128]{2,1,0:T(8,128)(4,1)S(1)} %get-tuple-element.10, f32[]{:T(128)} %bitcast.25, ...), kind=kLoop, calls=%fused_computation.218 | loop fusion | flops 3932160 | bytes 3407912 | tf_op jit(solution)/shard_map/mul | solution.py:95
  17.9 1.0 copy-done
  18.9 0.4 subtract_bitcast_fusion.11
  19.3 1.0 copy-done.1
  20.7 3.0 %collective-permute-start.1 = (f32[2,1,256,128]{3,2,1,0:T(8,128)S(1)}, f32[2,1,256,128]{3,2,1,0:T(8,128)S(1)}, u32[]{:S(2)}, u32[]{:S(2)}) collective-permute-start(f32[2,1,256,128]{3,2,1,0:T(8,128)S(1)} %slice.850), channel_id=1, source_target_pairs={{0,1},{1,2},{2,3},{3,4},{4,5},{5,6},{6,7},{7,8},{8,9},{9,10},{10,1... | collective-permute-start | bytes 786440 | tf_op jit(solution)/shard_map/ppermute | solution.py:14
  23.8 0.6 convolution_bitcast_fusion.10
  24.4 0.5 collective-permute-done.1
  24.9 0.7 subtract_bitcast_fusion.10
  25.6 0.4 fusion.2
  26.0 0.6 convolution_bitcast_fusion.11
  26.7 1.3 collective-permute-start.2
  28.6 5.8 %collective-permute-done.2 = f32[2,1,256,128]{3,2,1,0:T(8,128)S(1)} collective-permute-done((f32[2,1,256,128]{3,2,1,0:T(8,128)S(1)}, f32[2,1,256,128]{3,2,1,0:T(8,128)S(1)}, u32[]{:S(2)}, u32[]{:S(2)}) %collective-permute-start.2) | collective-permute-done | bytes 262176 | tf_op jit(solution)/shard_map/ppermute | solution.py:14
  35.2 7.4 %collective-permute-start.3 = (f32[2,1,256,128]{3,2,1,0:T(8,128)S(1)}, f32[2,1,256,128]{3,2,1,0:T(8,128)S(1)}, u32[]{:S(2)}, u32[]{:S(2)}) collective-permute-start(f32[2,1,256,128]{3,2,1,0:T(8,128)S(1)} %slice.874), channel_id=1, source_target_pairs={{0,1},{1,2},{2,3},{3,4},{4,5},{5,6},{6,7},{7,8},{8,9},{9,10},{10,1... | collective-permute-start | bytes 786440 | tf_op jit(solution)/shard_map/ppermute | solution.py:14
  42.7 0.6 convolution_bitcast_fusion.8
  43.3 0.5 collective-permute-done.3
  43.8 0.7 subtract_bitcast_fusion.8
  44.5 0.8 fusion.5
  45.3 0.6 convolution_bitcast_fusion.9
  46.0 1.3 collective-permute-start.4
  47.9 3.2 %collective-permute-done.4 = f32[2,1,256,128]{3,2,1,0:T(8,128)S(1)} collective-permute-done((f32[2,1,256,128]{3,2,1,0:T(8,128)S(1)}, f32[2,1,256,128]{3,2,1,0:T(8,128)S(1)}, u32[]{:S(2)}, u32[]{:S(2)}) %collective-permute-start.4) | collective-permute-done | bytes 262176 | tf_op jit(solution)/shard_map/ppermute | solution.py:14
  51.5 0.5 fusion.6
  52.1 7.6 %collective-permute-start.5 = (f32[2,1,256,128]{3,2,1,0:T(8,128)S(1)}, f32[2,1,256,128]{3,2,1,0:T(8,128)S(1)}, u32[]{:S(2)}, u32[]{:S(2)}) collective-permute-start(f32[2,1,256,128]{3,2,1,0:T(8,128)S(1)} %slice.898), channel_id=1, source_target_pairs={{0,1},{1,2},{2,3},{3,4},{4,5},{5,6},{6,7},{7,8},{8,9},{9,10},{10,1... | collective-permute-start | bytes 786440 | tf_op jit(solution)/shard_map/ppermute | solution.py:14
  59.7 0.6 convolution_bitcast_fusion.6
  60.7 0.7 subtract_bitcast_fusion.6
  61.4 1.3 fusion.8
  62.6 0.6 convolution_bitcast_fusion.7
  63.4 1.3 collective-permute-start.6
  65.3 3.2 %collective-permute-done.6 = f32[2,1,256,128]{3,2,1,0:T(8,128)S(1)} collective-permute-done((f32[2,1,256,128]{3,2,1,0:T(8,128)S(1)}, f32[2,1,256,128]{3,2,1,0:T(8,128)S(1)}, u32[]{:S(2)}, u32[]{:S(2)}) %collective-permute-start.6) | collective-permute-done | bytes 262176 | tf_op jit(solution)/shard_map/ppermute | solution.py:14
  68.7 0.6 fusion.9
  69.5 7.4 %collective-permute-start.7 = (f32[2,1,256,128]{3,2,1,0:T(8,128)S(1)}, f32[2,1,256,128]{3,2,1,0:T(8,128)S(1)}, u32[]{:S(2)}, u32[]{:S(2)}) collective-permute-start(f32[2,1,256,128]{3,2,1,0:T(8,128)S(1)} %slice.922), channel_id=1, source_target_pairs={{0,1},{1,2},{2,3},{3,4},{4,5},{5,6},{6,7},{7,8},{8,9},{9,10},{10,1... | collective-permute-start | bytes 786440 | tf_op jit(solution)/shard_map/ppermute | solution.py:14
  76.9 0.6 convolution_bitcast_fusion.4
  77.6 0.5 collective-permute-done.7
  78.1 0.7 subtract_bitcast_fusion.4
  78.8 1.2 fusion.11
  80.0 0.6 convolution_bitcast_fusion.5
  80.7 1.3 collective-permute-start.8
  82.6 3.2 %collective-permute-done.8 = f32[2,1,256,128]{3,2,1,0:T(8,128)S(1)} collective-permute-done((f32[2,1,256,128]{3,2,1,0:T(8,128)S(1)}, f32[2,1,256,128]{3,2,1,0:T(8,128)S(1)}, u32[]{:S(2)}, u32[]{:S(2)}) %collective-permute-start.8) | collective-permute-done | bytes 262176 | tf_op jit(solution)/shard_map/ppermute | solution.py:14
  86.2 0.6 fusion.12
  87.0 7.9 %collective-permute-start.9 = (f32[2,1,256,128]{3,2,1,0:T(8,128)S(1)}, f32[2,1,256,128]{3,2,1,0:T(8,128)S(1)}, u32[]{:S(2)}, u32[]{:S(2)}) collective-permute-start(f32[2,1,256,128]{3,2,1,0:T(8,128)S(1)} %slice.946), channel_id=1, source_target_pairs={{0,1},{1,2},{2,3},{3,4},{4,5},{5,6},{6,7},{7,8},{8,9},{9,10},{10,1... | collective-permute-start | bytes 786440 | tf_op jit(solution)/shard_map/ppermute | solution.py:14
  94.9 0.6 convolution_bitcast_fusion.2
  95.6 0.5 collective-permute-done.9
  96.1 0.7 subtract_bitcast_fusion.2
  96.8 1.0 fusion.14
  97.8 0.6 convolution_bitcast_fusion.3
  98.5 1.5 collective-permute-start.10
  100.6 3.0 %collective-permute-done.10 = f32[2,1,256,128]{3,2,1,0:T(8,128)S(1)} collective-permute-done((f32[2,1,256,128]{3,2,1,0:T(8,128)S(1)}, f32[2,1,256,128]{3,2,1,0:T(8,128)S(1)}, u32[]{:S(2)}, u32[]{:S(2)}) %collective-permute-start.10) | collective-permute-done | bytes 262176 | tf_op jit(solution)/shard_map/ppermute | solution.py:14
  103.9 0.8 fusion.15
  104.8 8.3 %collective-permute-start.11 = (f32[2,1,256,128]{3,2,1,0:T(8,128)S(1)}, f32[2,1,256,128]{3,2,1,0:T(8,128)S(1)}, u32[]{:S(2)}, u32[]{:S(2)}) collective-permute-start(f32[2,1,256,128]{3,2,1,0:T(8,128)S(1)} %slice.970), channel_id=1, source_target_pairs={{0,1},{1,2},{2,3},{3,4},{4,5},{5,6},{6,7},{7,8},{8,9},{9,10},{10,1... | collective-permute-start | bytes 786440 | tf_op jit(solution)/shard_map/ppermute | solution.py:14
  113.1 0.6 convolution_bitcast_fusion
  113.8 0.5 collective-permute-done.11
  114.3 0.7 subtract_bitcast_fusion
  115.0 1.4 fusion.17
  116.4 0.6 convolution_bitcast_fusion.1
  117.0 1.1 multiply_add_fusion
  118.2 7.0 %fusion.32 = f32[4,1,2,8,1,1]{3,1,5,4,2,0:T(1,128)S(1)} fusion(f32[2,4,8,4,4,256]{5,4,3,2,1,0:T(4,128)S(1)} %multiply_add_fusion, f32[4,4,4,256,1,1]{3,2,1,0,4,5:T(4,128)S(1)} %maximum_bitcast_fusion), kind=kOutput, calls=%fused_computation.61 | convolution fusion | flops 3145728 | bytes 1114368 | tf_op jit(solution)/shard_map/rcfmxy,cmxy->rmf/dot_general | solution.py:89
  125.2 33.2 %psum.7 = f32[2,4,8]{2,1,0:T(4,128)} all-reduce(f32[2,4,8]{2,1,0:T(4,128)S(1)} %fusion.84), channel_id=1, replica_groups=mesh['member'=2,'gx'=16] {'gx'}, use_global_device_ids=true, to_apply=%region_0.1 | all-reduce | flops 64 | bytes 512 | tf_op jit(solution)/shard_map/psum | solution.py:136
  (131 shorter events, 8.1 us)
Async XLA Ops:
  1.6 3.0 %copy-start.9 = (f32[2]{0:T(128)S(1)}, f32[2]{0:T(128)}, u32[]{:S(2)}) copy-start(f32[2]{0:T(128)} %param.14) | copy-start | bytes 28
  1.6 6.2 %copy-start.10 = (f32[2]{0:T(128)S(1)}, f32[2]{0:T(128)}, u32[]{:S(2)}) copy-start(f32[2]{0:T(128)} %param.15) | copy-start | bytes 28
  1.6 6.7 %copy-start.11 = (f32[2]{0:T(128)S(1)}, f32[2]{0:T(128)}, u32[]{:S(2)}) copy-start(f32[2]{0:T(128)} %param.16) | copy-start | bytes 28
  1.6 7.3 %copy-start.8 = (f32[4]{0:T(128)S(1)}, f32[4]{0:T(128)}, u32[]{:S(2)}) copy-start(f32[4]{0:T(128)} %param.13) | copy-start | bytes 52
  1.7 8.0 %copy-start.12 = (f32[8]{0:T(128)S(1)}, f32[8]{0:T(128)}, u32[]{:S(2)}) copy-start(f32[8]{0:T(128)} %param.17) | copy-start | bytes 100
  1.7 8.2 %copy-start.7 = (f32[4,4,4,256]{3,2,1,0:T(4,128)S(1)}, f32[4,4,4,256]{3,2,1,0:T(4,128)}, u32[]{:S(2)}) copy-start(f32[4,4,4,256]{3,2,1,0:T(4,128)} %param.19) | copy-start | bytes 196612
  1.7 9.7 %copy-start.5 = (s32[4,256,128]{2,1,0:T(8,128)S(1)}, s32[4,256,128]{2,1,0:T(8,128)}, u32[]{:S(2)}) copy-start(s32[4,256,128]{2,1,0:T(8,128)} %param.12) | copy-start | bytes 1572868
  1.7 17.2 %collective-permute-start = (f32[2,1,256,128]{3,2,1,0:T(8,128)S(1)}, f32[2,1,256,128]{3,2,1,0:T(8,128)S(1)}, u32[]{:S(2)}, u32[]{:S(2)}) collective-permute-start(f32[2,1,256,128]{3,2,1,0:T(8,128)S(1)} %slice.656), channel_id=1, source_target_pairs={{1,0},{2,1},{3,2},{4,3},{5,4},{6,5},{7,6},{8,7},{9,8},{10,9},{11,1... | collective-permute-start | bytes 786440 | tf_op jit(solution)/shard_map/ppermute | solution.py:14
  17.4 1.4 copy-start
  18.9 1.4 copy-start.1
  20.6 3.2 %copy-start.6 = (s32[4]{0:T(128)S(1)}, s32[4]{0:T(128)}, u32[]{:S(2)}) copy-start(s32[4]{0:T(128)} %param.18) | copy-start | bytes 52
  20.7 4.2 %collective-permute-start.1 = (f32[2,1,256,128]{3,2,1,0:T(8,128)S(1)}, f32[2,1,256,128]{3,2,1,0:T(8,128)S(1)}, u32[]{:S(2)}, u32[]{:S(2)}) collective-permute-start(f32[2,1,256,128]{3,2,1,0:T(8,128)S(1)} %slice.850), channel_id=1, source_target_pairs={{0,1},{1,2},{2,3},{3,4},{4,5},{5,6},{6,7},{7,8},{8,9},{9,10},{10,1... | collective-permute-start | bytes 786440 | tf_op jit(solution)/shard_map/ppermute | solution.py:14
  26.7 7.7 %collective-permute-start.2 = (f32[2,1,256,128]{3,2,1,0:T(8,128)S(1)}, f32[2,1,256,128]{3,2,1,0:T(8,128)S(1)}, u32[]{:S(2)}, u32[]{:S(2)}) collective-permute-start(f32[2,1,256,128]{3,2,1,0:T(8,128)S(1)} %slice.863), channel_id=1, source_target_pairs={{1,0},{2,1},{3,2},{4,3},{5,4},{6,5},{7,6},{8,7},{9,8},{10,9},{11,1... | collective-permute-start | bytes 786440 | tf_op jit(solution)/shard_map/ppermute | solution.py:14
  35.2 8.6 %collective-permute-start.3 = (f32[2,1,256,128]{3,2,1,0:T(8,128)S(1)}, f32[2,1,256,128]{3,2,1,0:T(8,128)S(1)}, u32[]{:S(2)}, u32[]{:S(2)}) collective-permute-start(f32[2,1,256,128]{3,2,1,0:T(8,128)S(1)} %slice.874), channel_id=1, source_target_pairs={{0,1},{1,2},{2,3},{3,4},{4,5},{5,6},{6,7},{7,8},{8,9},{9,10},{10,1... | collective-permute-start | bytes 786440 | tf_op jit(solution)/shard_map/ppermute | solution.py:14
  46.0 5.1 %collective-permute-start.4 = (f32[2,1,256,128]{3,2,1,0:T(8,128)S(1)}, f32[2,1,256,128]{3,2,1,0:T(8,128)S(1)}, u32[]{:S(2)}, u32[]{:S(2)}) collective-permute-start(f32[2,1,256,128]{3,2,1,0:T(8,128)S(1)} %slice.887), channel_id=1, source_target_pairs={{1,0},{2,1},{3,2},{4,3},{5,4},{6,5},{7,6},{8,7},{9,8},{10,9},{11,1... | collective-permute-start | bytes 786440 | tf_op jit(solution)/shard_map/ppermute | solution.py:14
  52.1 8.6 %collective-permute-start.5 = (f32[2,1,256,128]{3,2,1,0:T(8,128)S(1)}, f32[2,1,256,128]{3,2,1,0:T(8,128)S(1)}, u32[]{:S(2)}, u32[]{:S(2)}) collective-permute-start(f32[2,1,256,128]{3,2,1,0:T(8,128)S(1)} %slice.898), channel_id=1, source_target_pairs={{0,1},{1,2},{2,3},{3,4},{4,5},{5,6},{6,7},{7,8},{8,9},{9,10},{10,1... | collective-permute-start | bytes 786440 | tf_op jit(solution)/shard_map/ppermute | solution.py:14
  63.4 5.1 %collective-permute-start.6 = (f32[2,1,256,128]{3,2,1,0:T(8,128)S(1)}, f32[2,1,256,128]{3,2,1,0:T(8,128)S(1)}, u32[]{:S(2)}, u32[]{:S(2)}) collective-permute-start(f32[2,1,256,128]{3,2,1,0:T(8,128)S(1)} %slice.911), channel_id=1, source_target_pairs={{1,0},{2,1},{3,2},{4,3},{5,4},{6,5},{7,6},{8,7},{9,8},{10,9},{11,1... | collective-permute-start | bytes 786440 | tf_op jit(solution)/shard_map/ppermute | solution.py:14
  69.5 8.6 %collective-permute-start.7 = (f32[2,1,256,128]{3,2,1,0:T(8,128)S(1)}, f32[2,1,256,128]{3,2,1,0:T(8,128)S(1)}, u32[]{:S(2)}, u32[]{:S(2)}) collective-permute-start(f32[2,1,256,128]{3,2,1,0:T(8,128)S(1)} %slice.922), channel_id=1, source_target_pairs={{0,1},{1,2},{2,3},{3,4},{4,5},{5,6},{6,7},{7,8},{8,9},{9,10},{10,1... | collective-permute-start | bytes 786440 | tf_op jit(solution)/shard_map/ppermute | solution.py:14
  80.7 5.1 %collective-permute-start.8 = (f32[2,1,256,128]{3,2,1,0:T(8,128)S(1)}, f32[2,1,256,128]{3,2,1,0:T(8,128)S(1)}, u32[]{:S(2)}, u32[]{:S(2)}) collective-permute-start(f32[2,1,256,128]{3,2,1,0:T(8,128)S(1)} %slice.935), channel_id=1, source_target_pairs={{1,0},{2,1},{3,2},{4,3},{5,4},{6,5},{7,6},{8,7},{9,8},{10,9},{11,1... | collective-permute-start | bytes 786440 | tf_op jit(solution)/shard_map/ppermute | solution.py:14
  87.0 9.1 %collective-permute-start.9 = (f32[2,1,256,128]{3,2,1,0:T(8,128)S(1)}, f32[2,1,256,128]{3,2,1,0:T(8,128)S(1)}, u32[]{:S(2)}, u32[]{:S(2)}) collective-permute-start(f32[2,1,256,128]{3,2,1,0:T(8,128)S(1)} %slice.946), channel_id=1, source_target_pairs={{0,1},{1,2},{2,3},{3,4},{4,5},{5,6},{6,7},{7,8},{8,9},{9,10},{10,1... | collective-permute-start | bytes 786440 | tf_op jit(solution)/shard_map/ppermute | solution.py:14
  98.5 5.1 %collective-permute-start.10 = (f32[2,1,256,128]{3,2,1,0:T(8,128)S(1)}, f32[2,1,256,128]{3,2,1,0:T(8,128)S(1)}, u32[]{:S(2)}, u32[]{:S(2)}) collective-permute-start(f32[2,1,256,128]{3,2,1,0:T(8,128)S(1)} %slice.959), channel_id=1, source_target_pairs={{1,0},{2,1},{3,2},{4,3},{5,4},{6,5},{7,6},{8,7},{9,8},{10,9},{11,1... | collective-permute-start | bytes 786440 | tf_op jit(solution)/shard_map/ppermute | solution.py:14
  104.7 9.6 %copy-start.2 = (f32[3,4,256,128]{3,2,1,0:T(8,128)}, f32[3,4,256,128]{3,2,1,0:T(8,128)S(1)}, u32[]{:S(2)}) copy-start(f32[3,4,256,128]{3,2,1,0:T(8,128)S(1)} %fusion.15) | copy-start | bytes 4718596
  104.8 9.5 %collective-permute-start.11 = (f32[2,1,256,128]{3,2,1,0:T(8,128)S(1)}, f32[2,1,256,128]{3,2,1,0:T(8,128)S(1)}, u32[]{:S(2)}, u32[]{:S(2)}) collective-permute-start(f32[2,1,256,128]{3,2,1,0:T(8,128)S(1)} %slice.970), channel_id=1, source_target_pairs={{0,1},{1,2},{2,3},{3,4},{4,5},{5,6},{6,7},{7,8},{8,9},{9,10},{10,1... | collective-permute-start | bytes 786440 | tf_op jit(solution)/shard_map/ppermute | solution.py:14
  116.4 8.8 %copy-start.3 = (f32[3,4,256,128]{3,2,1,0:T(8,128)}, f32[3,4,256,128]{3,2,1,0:T(8,128)S(1)}, u32[]{:S(2)}) copy-start(f32[3,4,256,128]{3,2,1,0:T(8,128)S(1)} %fusion.17) | copy-start | bytes 4718596
  118.2 40.2 %copy-start.4 = (f32[2,4,8,4,4,256]{5,4,3,2,1,0:T(4,128)}, f32[2,4,8,4,4,256]{5,4,3,2,1,0:T(4,128)S(1)}, u32[]{:S(2)}) copy-start(f32[2,4,8,4,4,256]{5,4,3,2,1,0:T(4,128)S(1)} %multiply_add_fusion) | copy-start | bytes 3145732
where the time goes:
time: 159 us; the launch traced here: 158 us
  starting transfers between devices  49.9 us (31%)
  blocking collectives  33.2 us (21%)
  other arithmetic  22.6 us (14%)
  waiting for transfers between devices  21 us (13%)
  matrix products  13.9 us (9%)
  local copies, waits for them, and re-layouts  12.2 us (8%)
  between operations  5.55 us (3%)
    ppermute x12, starting transfers between devices, shifted(): lax.ppermute(value, axis, [(source, source + steps) for source in range(f...  49.9 us
    psum x1, blocking collectives, on_device(): intersection = lax.psum(partial_value, 'gx')  33.2 us
    ppermute x12, waiting for transfers between devices, shifted(): lax.ppermute(value, axis, [(source, source + steps) for source in range(f...  21 us
    dot_general x1, matrix products, project(): jnp.einsum('rcfmxy,cmxy->rmf', monitors, pairing, precision=lax.Precision...  6.99 us
    add x6, other arithmetic, pole_update(): e_field = e_field + step_e * (curl_field - current)  5.96 us
    mul x1, other arithmetic, pole_update(): current = retain * current + pulling * e_field - spring * polarized  4.4 us
    another operation x6, other arithmetic, curl_h(): return jnp.stack([first, second, third])  4.26 us
    dot_general x6, matrix products, record(): jnp.einsum('cxyz,zm->cmxy', h_field[:2], select, precision=lax.Precision....  3.47 us
  transfers between devices with their start and end apart: 12, of which 11 were waited for; matrix products, arithmetic and copies ran while one was open for 11% of the time, Pallas kernels for 0%

commit v1 on v0

--- a/solution.py
+++ b/solution.py
@@ -133,7 +133,7 @@
         monitors = record(monitors, electric, magnetic, select, frequencies, step)
     scale = 1.0 / math.sqrt(4.0 * slab_cells * lax.axis_size("gx") * width_y)
     partial_value = project(monitors, mode_fields, scale)
-    intersection = lax.psum(partial_value, "gx")
+    intersection = jnp.sum(lax.all_gather(partial_value, "gx"), axis=0)
     return (electric, magnetic, monitors, intersection)
 
 

time: 159 us -> 152 us (0.956)
  blocking collectives: 33.2 us -> 25.5 us
    psum x1 -> x0, blocking collectives: 33.2 us -> none  [on_device(): intersection = lax.psum(partial_value, 'gx')]
    all_gather x0 -> x1, blocking collectives: none -> 25.5 us  [on_device(): intersection = jnp.sum(lax.all_gather(partial_value, 'gx'), axis=0)]
where the time goes in v1:
time: 152 us; the launch traced here: 151 us
  starting transfers between devices  49.9 us (33%)
  blocking collectives  25.5 us (17%)
  other arithmetic  23.2 us (15%)
  waiting for transfers between devices  21 us (14%)
  matrix products  13.9 us (9%)
  local copies, waits for them, and re-layouts  12.2 us (8%)
  between operations  5.55 us (4%)
    ppermute x12, starting transfers between devices, shifted(): lax.ppermute(value, axis, [(source, source + steps) for source in range(f...  49.9 us
    all_gather x1, blocking collectives, on_device(): intersection = jnp.sum(lax.all_gather(partial_value, 'gx'), axis=0)  25.5 us
    ppermute x12, waiting for transfers between devices, shifted(): lax.ppermute(value, axis, [(source, source + steps) for source in range(f...  21 us
    dot_general x1, matrix products, project(): jnp.einsum('rcfmxy,cmxy->rmf', monitors, pairing, precision=lax.Precision...  6.99 us
    add x6, other arithmetic, pole_update(): e_field = e_field + step_e * (curl_field - current)  5.96 us
    mul x1, other arithmetic, pole_update(): current = retain * current + pulling * e_field - spring * polarized  4.4 us
    another operation x6, other arithmetic, curl_h(): return jnp.stack([first, second, third])  4.26 us
    dot_general x6, matrix products, record(): jnp.einsum('cxyz,zm->cmxy', h_field[:2], select, precision=lax.Precision....  3.47 us
  transfers between devices with their start and end apart: 12, of which 11 were waited for; matrix products, arithmetic and copies ran while one was open for 11% of the time, Pallas kernels for 0%

profile of v1, /device:TPU:0, one launch (start us, length us, event | category | flops | bytes accessed | tf_op | source)
XLA Modules:
  0.0 151.3 jit_solution(5656615637664879562)
XLA Ops:
  0.6 1.0 slice.656
  1.7 1.4 collective-permute-start
  3.1 1.5 slice_bitcast_fusion.35
  4.6 0.6 fusion.102
  7.8 0.6 fusion.103
  8.4 0.6 fusion.101
  9.0 0.7 fusion.100
  11.3 1.6 %subtract_divide_fusion = (f32[4,256,128]{2,1,0:T(8,128)S(1)}, pred[4,256,128]{2,1,0:T(8,128)(4,1)S(1)}, pred[4,256,128]{2,1,0:T(8,128)(4,1)S(1)}) fusion(f32[]{:T(128)} %bitcast.25, f32[]{:T(128)} %bitcast.24, s32[4,256,128]{2,1,0:T(8,128)S(1)} %copy-done.5), kind=kLoop, calls=%fused_computation.181 | loop fusion | flops 1179648 | bytes 1310728 | tf_op jit(solution)/shard_map/div | solution.py:68
  13.0 4.4 %broadcast_multiply_fusion.2 = (f32[4,256,128]{2,1,0:T(8,128)S(1)}, f32[4,256,128]{2,1,0:T(8,128)S(1)}, f32[4,256,128]{2,1,0:T(8,128)S(1)}, f32[4,256,128]{2,1,0:T(8,128)S(1)}, f32[4,256,128]{2,1,0:T(8,128)S(1)}) fusion(pred[4,256,128]{2,1,0:T(8,128)(4,1)S(1)} %get-tuple-element.10, f32[]{:T(128)} %bitcast.25, ...), kind=kLoop, calls=%fused_computation.218 | loop fusion | flops 3932160 | bytes 3407912 | tf_op jit(solution)/shard_map/mul | solution.py:95
  17.9 1.0 copy-done
  19.3 1.0 copy-done.1
  20.7 3.0 %collective-permute-start.1 = (f32[2,1,256,128]{3,2,1,0:T(8,128)S(1)}, f32[2,1,256,128]{3,2,1,0:T(8,128)S(1)}, u32[]{:S(2)}, u32[]{:S(2)}) collective-permute-start(f32[2,1,256,128]{3,2,1,0:T(8,128)S(1)} %slice.850), channel_id=1, source_target_pairs={{0,1},{1,2},{2,3},{3,4},{4,5},{5,6},{6,7},{7,8},{8,9},{9,10},{10,1... | collective-permute-start | bytes 786440 | tf_op jit(solution)/shard_map/ppermute | solution.py:14
  23.8 0.6 convolution_bitcast_fusion.10
  24.4 0.5 collective-permute-done.1
  24.9 0.7 subtract_bitcast_fusion.10
  25.6 0.4 fusion.2
  26.0 0.6 convolution_bitcast_fusion.11
  26.7 1.3 collective-permute-start.2
  28.6 5.8 %collective-permute-done.2 = f32[2,1,256,128]{3,2,1,0:T(8,128)S(1)} collective-permute-done((f32[2,1,256,128]{3,2,1,0:T(8,128)S(1)}, f32[2,1,256,128]{3,2,1,0:T(8,128)S(1)}, u32[]{:S(2)}, u32[]{:S(2)}) %collective-permute-start.2) | collective-permute-done | bytes 262176 | tf_op jit(solution)/shard_map/ppermute | solution.py:14
  35.2 7.4 %collective-permute-start.3 = (f32[2,1,256,128]{3,2,1,0:T(8,128)S(1)}, f32[2,1,256,128]{3,2,1,0:T(8,128)S(1)}, u32[]{:S(2)}, u32[]{:S(2)}) collective-permute-start(f32[2,1,256,128]{3,2,1,0:T(8,128)S(1)} %slice.874), channel_id=1, source_target_pairs={{0,1},{1,2},{2,3},{3,4},{4,5},{5,6},{6,7},{7,8},{8,9},{9,10},{10,1... | collective-permute-start | bytes 786440 | tf_op jit(solution)/shard_map/ppermute | solution.py:14
  42.7 0.6 convolution_bitcast_fusion.8
  43.3 0.5 collective-permute-done.3
  43.8 0.7 subtract_bitcast_fusion.8
  44.5 0.8 fusion.5
  45.3 0.6 convolution_bitcast_fusion.9
  46.0 1.3 collective-permute-start.4
  47.9 3.2 %collective-permute-done.4 = f32[2,1,256,128]{3,2,1,0:T(8,128)S(1)} collective-permute-done((f32[2,1,256,128]{3,2,1,0:T(8,128)S(1)}, f32[2,1,256,128]{3,2,1,0:T(8,128)S(1)}, u32[]{:S(2)}, u32[]{:S(2)}) %collective-permute-start.4) | collective-permute-done | bytes 262176 | tf_op jit(solution)/shard_map/ppermute | solution.py:14
  51.5 0.5 fusion.6
  52.1 7.6 %collective-permute-start.5 = (f32[2,1,256,128]{3,2,1,0:T(8,128)S(1)}, f32[2,1,256,128]{3,2,1,0:T(8,128)S(1)}, u32[]{:S(2)}, u32[]{:S(2)}) collective-permute-start(f32[2,1,256,128]{3,2,1,0:T(8,128)S(1)} %slice.898), channel_id=1, source_target_pairs={{0,1},{1,2},{2,3},{3,4},{4,5},{5,6},{6,7},{7,8},{8,9},{9,10},{10,1... | collective-permute-start | bytes 786440 | tf_op jit(solution)/shard_map/ppermute | solution.py:14
  59.7 0.6 convolution_bitcast_fusion.6
  60.7 0.7 subtract_bitcast_fusion.6
  61.4 1.3 fusion.8
  62.6 0.6 convolution_bitcast_fusion.7
  63.4 1.3 collective-permute-start.6
  65.3 3.2 %collective-permute-done.6 = f32[2,1,256,128]{3,2,1,0:T(8,128)S(1)} collective-permute-done((f32[2,1,256,128]{3,2,1,0:T(8,128)S(1)}, f32[2,1,256,128]{3,2,1,0:T(8,128)S(1)}, u32[]{:S(2)}, u32[]{:S(2)}) %collective-permute-start.6) | collective-permute-done | bytes 262176 | tf_op jit(solution)/shard_map/ppermute | solution.py:14
  68.7 0.6 fusion.9
  69.5 7.4 %collective-permute-start.7 = (f32[2,1,256,128]{3,2,1,0:T(8,128)S(1)}, f32[2,1,256,128]{3,2,1,0:T(8,128)S(1)}, u32[]{:S(2)}, u32[]{:S(2)}) collective-permute-start(f32[2,1,256,128]{3,2,1,0:T(8,128)S(1)} %slice.922), channel_id=1, source_target_pairs={{0,1},{1,2},{2,3},{3,4},{4,5},{5,6},{6,7},{7,8},{8,9},{9,10},{10,1... | collective-permute-start | bytes 786440 | tf_op jit(solution)/shard_map/ppermute | solution.py:14
  76.9 0.6 convolution_bitcast_fusion.4
  77.6 0.5 collective-permute-done.7
  78.1 0.7 subtract_bitcast_fusion.4
  78.8 1.2 fusion.11
  80.0 0.6 convolution_bitcast_fusion.5
  80.7 1.3 collective-permute-start.8
  82.6 3.2 %collective-permute-done.8 = f32[2,1,256,128]{3,2,1,0:T(8,128)S(1)} collective-permute-done((f32[2,1,256,128]{3,2,1,0:T(8,128)S(1)}, f32[2,1,256,128]{3,2,1,0:T(8,128)S(1)}, u32[]{:S(2)}, u32[]{:S(2)}) %collective-permute-start.8) | collective-permute-done | bytes 262176 | tf_op jit(solution)/shard_map/ppermute | solution.py:14
  86.2 0.6 fusion.12
  87.0 7.9 %collective-permute-start.9 = (f32[2,1,256,128]{3,2,1,0:T(8,128)S(1)}, f32[2,1,256,128]{3,2,1,0:T(8,128)S(1)}, u32[]{:S(2)}, u32[]{:S(2)}) collective-permute-start(f32[2,1,256,128]{3,2,1,0:T(8,128)S(1)} %slice.946), channel_id=1, source_target_pairs={{0,1},{1,2},{2,3},{3,4},{4,5},{5,6},{6,7},{7,8},{8,9},{9,10},{10,1... | collective-permute-start | bytes 786440 | tf_op jit(solution)/shard_map/ppermute | solution.py:14
  94.9 0.6 convolution_bitcast_fusion.2
  95.6 0.5 collective-permute-done.9
  96.1 0.7 subtract_bitcast_fusion.2
  96.8 1.0 fusion.14
  97.8 0.6 convolution_bitcast_fusion.3
  98.5 1.5 collective-permute-start.10
  100.6 3.0 %collective-permute-done.10 = f32[2,1,256,128]{3,2,1,0:T(8,128)S(1)} collective-permute-done((f32[2,1,256,128]{3,2,1,0:T(8,128)S(1)}, f32[2,1,256,128]{3,2,1,0:T(8,128)S(1)}, u32[]{:S(2)}, u32[]{:S(2)}) %collective-permute-start.10) | collective-permute-done | bytes 262176 | tf_op jit(solution)/shard_map/ppermute | solution.py:14
  103.9 0.8 fusion.15
  104.8 8.3 %collective-permute-start.11 = (f32[2,1,256,128]{3,2,1,0:T(8,128)S(1)}, f32[2,1,256,128]{3,2,1,0:T(8,128)S(1)}, u32[]{:S(2)}, u32[]{:S(2)}) collective-permute-start(f32[2,1,256,128]{3,2,1,0:T(8,128)S(1)} %slice.970), channel_id=1, source_target_pairs={{0,1},{1,2},{2,3},{3,4},{4,5},{5,6},{6,7},{7,8},{8,9},{9,10},{10,1... | collective-permute-start | bytes 786440 | tf_op jit(solution)/shard_map/ppermute | solution.py:14
  113.1 0.6 convolution_bitcast_fusion
  113.8 0.5 collective-permute-done.11
  114.3 0.7 subtract_bitcast_fusion
  115.0 1.4 fusion.17
  116.4 0.6 convolution_bitcast_fusion.1
  117.0 1.1 multiply_add_fusion
  118.2 7.0 %fusion.32 = f32[4,1,2,8,1,1]{3,1,5,4,2,0:T(1,128)S(1)} fusion(f32[2,4,8,4,4,256]{5,4,3,2,1,0:T(4,128)S(1)} %multiply_add_fusion, f32[4,4,4,256,1,1]{3,2,1,0,4,5:T(4,128)S(1)} %maximum_bitcast_fusion), kind=kOutput, calls=%fused_computation.61 | convolution fusion | flops 3145728 | bytes 1114368 | tf_op jit(solution)/shard_map/rcfmxy,cmxy->rmf/dot_general | solution.py:89
  125.2 25.5 %all-gather = f32[32,4,8]{2,1,0:T(4,128)S(1)} all-gather(f32[2,4,8]{2,1,0:T(4,128)S(1)} %fusion.84), channel_id=2, replica_groups=mesh['member'=2,'gx'=16] {'gx'}, dimensions={0}, use_global_device_ids=true | all-gather | bytes 4352 | tf_op jit(solution)/shard_map/all_gather | solution.py:136
  150.7 0.6 reduce_sum.9
  (132 shorter events, 8.4 us)
Async XLA Ops:
  1.6 3.0 %copy-start.9 = (f32[2]{0:T(128)S(1)}, f32[2]{0:T(128)}, u32[]{:S(2)}) copy-start(f32[2]{0:T(128)} %param.14) | copy-start | bytes 28
  1.6 6.2 %copy-start.10 = (f32[2]{0:T(128)S(1)}, f32[2]{0:T(128)}, u32[]{:S(2)}) copy-start(f32[2]{0:T(128)} %param.15) | copy-start | bytes 28
  1.6 6.7 %copy-start.11 = (f32[2]{0:T(128)S(1)}, f32[2]{0:T(128)}, u32[]{:S(2)}) copy-start(f32[2]{0:T(128)} %param.16) | copy-start | bytes 28
  1.6 7.3 %copy-start.8 = (f32[4]{0:T(128)S(1)}, f32[4]{0:T(128)}, u32[]{:S(2)}) copy-start(f32[4]{0:T(128)} %param.13) | copy-start | bytes 52
  1.7 8.0 %copy-start.12 = (f32[8]{0:T(128)S(1)}, f32[8]{0:T(128)}, u32[]{:S(2)}) copy-start(f32[8]{0:T(128)} %param.17) | copy-start | bytes 100
  1.7 8.2 %copy-start.7 = (f32[4,4,4,256]{3,2,1,0:T(4,128)S(1)}, f32[4,4,4,256]{3,2,1,0:T(4,128)}, u32[]{:S(2)}) copy-start(f32[4,4,4,256]{3,2,1,0:T(4,128)} %param.19) | copy-start | bytes 196612
  1.7 9.7 %copy-start.5 = (s32[4,256,128]{2,1,0:T(8,128)S(1)}, s32[4,256,128]{2,1,0:T(8,128)}, u32[]{:S(2)}) copy-start(s32[4,256,128]{2,1,0:T(8,128)} %param.12) | copy-start | bytes 1572868
  1.7 17.2 %collective-permute-start = (f32[2,1,256,128]{3,2,1,0:T(8,128)S(1)}, f32[2,1,256,128]{3,2,1,0:T(8,128)S(1)}, u32[]{:S(2)}, u32[]{:S(2)}) collective-permute-start(f32[2,1,256,128]{3,2,1,0:T(8,128)S(1)} %slice.656), channel_id=1, source_target_pairs={{1,0},{2,1},{3,2},{4,3},{5,4},{6,5},{7,6},{8,7},{9,8},{10,9},{11,1... | collective-permute-start | bytes 786440 | tf_op jit(solution)/shard_map/ppermute | solution.py:14
  17.4 1.4 copy-start
  18.9 1.4 copy-start.1
  20.6 3.2 %copy-start.6 = (s32[4]{0:T(128)S(1)}, s32[4]{0:T(128)}, u32[]{:S(2)}) copy-start(s32[4]{0:T(128)} %param.18) | copy-start | bytes 52
  20.7 4.2 %collective-permute-start.1 = (f32[2,1,256,128]{3,2,1,0:T(8,128)S(1)}, f32[2,1,256,128]{3,2,1,0:T(8,128)S(1)}, u32[]{:S(2)}, u32[]{:S(2)}) collective-permute-start(f32[2,1,256,128]{3,2,1,0:T(8,128)S(1)} %slice.850), channel_id=1, source_target_pairs={{0,1},{1,2},{2,3},{3,4},{4,5},{5,6},{6,7},{7,8},{8,9},{9,10},{10,1... | collective-permute-start | bytes 786440 | tf_op jit(solution)/shard_map/ppermute | solution.py:14
  26.7 7.7 %collective-permute-start.2 = (f32[2,1,256,128]{3,2,1,0:T(8,128)S(1)}, f32[2,1,256,128]{3,2,1,0:T(8,128)S(1)}, u32[]{:S(2)}, u32[]{:S(2)}) collective-permute-start(f32[2,1,256,128]{3,2,1,0:T(8,128)S(1)} %slice.863), channel_id=1, source_target_pairs={{1,0},{2,1},{3,2},{4,3},{5,4},{6,5},{7,6},{8,7},{9,8},{10,9},{11,1... | collective-permute-start | bytes 786440 | tf_op jit(solution)/shard_map/ppermute | solution.py:14
  35.2 8.6 %collective-permute-start.3 = (f32[2,1,256,128]{3,2,1,0:T(8,128)S(1)}, f32[2,1,256,128]{3,2,1,0:T(8,128)S(1)}, u32[]{:S(2)}, u32[]{:S(2)}) collective-permute-start(f32[2,1,256,128]{3,2,1,0:T(8,128)S(1)} %slice.874), channel_id=1, source_target_pairs={{0,1},{1,2},{2,3},{3,4},{4,5},{5,6},{6,7},{7,8},{8,9},{9,10},{10,1... | collective-permute-start | bytes 786440 | tf_op jit(solution)/shard_map/ppermute | solution.py:14
  46.0 5.1 %collective-permute-start.4 = (f32[2,1,256,128]{3,2,1,0:T(8,128)S(1)}, f32[2,1,256,128]{3,2,1,0:T(8,128)S(1)}, u32[]{:S(2)}, u32[]{:S(2)}) collective-permute-start(f32[2,1,256,128]{3,2,1,0:T(8,128)S(1)} %slice.887), channel_id=1, source_target_pairs={{1,0},{2,1},{3,2},{4,3},{5,4},{6,5},{7,6},{8,7},{9,8},{10,9},{11,1... | collective-permute-start | bytes 786440 | tf_op jit(solution)/shard_map/ppermute | solution.py:14
  52.1 8.6 %collective-permute-start.5 = (f32[2,1,256,128]{3,2,1,0:T(8,128)S(1)}, f32[2,1,256,128]{3,2,1,0:T(8,128)S(1)}, u32[]{:S(2)}, u32[]{:S(2)}) collective-permute-start(f32[2,1,256,128]{3,2,1,0:T(8,128)S(1)} %slice.898), channel_id=1, source_target_pairs={{0,1},{1,2},{2,3},{3,4},{4,5},{5,6},{6,7},{7,8},{8,9},{9,10},{10,1... | collective-permute-start | bytes 786440 | tf_op jit(solution)/shard_map/ppermute | solution.py:14
  63.4 5.1 %collective-permute-start.6 = (f32[2,1,256,128]{3,2,1,0:T(8,128)S(1)}, f32[2,1,256,128]{3,2,1,0:T(8,128)S(1)}, u32[]{:S(2)}, u32[]{:S(2)}) collective-permute-start(f32[2,1,256,128]{3,2,1,0:T(8,128)S(1)} %slice.911), channel_id=1, source_target_pairs={{1,0},{2,1},{3,2},{4,3},{5,4},{6,5},{7,6},{8,7},{9,8},{10,9},{11,1... | collective-permute-start | bytes 786440 | tf_op jit(solution)/shard_map/ppermute | solution.py:14
  69.5 8.6 %collective-permute-start.7 = (f32[2,1,256,128]{3,2,1,0:T(8,128)S(1)}, f32[2,1,256,128]{3,2,1,0:T(8,128)S(1)}, u32[]{:S(2)}, u32[]{:S(2)}) collective-permute-start(f32[2,1,256,128]{3,2,1,0:T(8,128)S(1)} %slice.922), channel_id=1, source_target_pairs={{0,1},{1,2},{2,3},{3,4},{4,5},{5,6},{6,7},{7,8},{8,9},{9,10},{10,1... | collective-permute-start | bytes 786440 | tf_op jit(solution)/shard_map/ppermute | solution.py:14
  80.7 5.1 %collective-permute-start.8 = (f32[2,1,256,128]{3,2,1,0:T(8,128)S(1)}, f32[2,1,256,128]{3,2,1,0:T(8,128)S(1)}, u32[]{:S(2)}, u32[]{:S(2)}) collective-permute-start(f32[2,1,256,128]{3,2,1,0:T(8,128)S(1)} %slice.935), channel_id=1, source_target_pairs={{1,0},{2,1},{3,2},{4,3},{5,4},{6,5},{7,6},{8,7},{9,8},{10,9},{11,1... | collective-permute-start | bytes 786440 | tf_op jit(solution)/shard_map/ppermute | solution.py:14
  87.0 9.1 %collective-permute-start.9 = (f32[2,1,256,128]{3,2,1,0:T(8,128)S(1)}, f32[2,1,256,128]{3,2,1,0:T(8,128)S(1)}, u32[]{:S(2)}, u32[]{:S(2)}) collective-permute-start(f32[2,1,256,128]{3,2,1,0:T(8,128)S(1)} %slice.946), channel_id=1, source_target_pairs={{0,1},{1,2},{2,3},{3,4},{4,5},{5,6},{6,7},{7,8},{8,9},{9,10},{10,1... | collective-permute-start | bytes 786440 | tf_op jit(solution)/shard_map/ppermute | solution.py:14
  98.5 5.1 %collective-permute-start.10 = (f32[2,1,256,128]{3,2,1,0:T(8,128)S(1)}, f32[2,1,256,128]{3,2,1,0:T(8,128)S(1)}, u32[]{:S(2)}, u32[]{:S(2)}) collective-permute-start(f32[2,1,256,128]{3,2,1,0:T(8,128)S(1)} %slice.959), channel_id=1, source_target_pairs={{1,0},{2,1},{3,2},{4,3},{5,4},{6,5},{7,6},{8,7},{9,8},{10,9},{11,1... | collective-permute-start | bytes 786440 | tf_op jit(solution)/shard_map/ppermute | solution.py:14
  104.7 9.6 %copy-start.2 = (f32[3,4,256,128]{3,2,1,0:T(8,128)}, f32[3,4,256,128]{3,2,1,0:T(8,128)S(1)}, u32[]{:S(2)}) copy-start(f32[3,4,256,128]{3,2,1,0:T(8,128)S(1)} %fusion.15) | copy-start | bytes 4718596
  104.8 9.5 %collective-permute-start.11 = (f32[2,1,256,128]{3,2,1,0:T(8,128)S(1)}, f32[2,1,256,128]{3,2,1,0:T(8,128)S(1)}, u32[]{:S(2)}, u32[]{:S(2)}) collective-permute-start(f32[2,1,256,128]{3,2,1,0:T(8,128)S(1)} %slice.970), channel_id=1, source_target_pairs={{0,1},{1,2},{2,3},{3,4},{4,5},{5,6},{6,7},{7,8},{8,9},{9,10},{10,1... | collective-permute-start | bytes 786440 | tf_op jit(solution)/shard_map/ppermute | solution.py:14
  116.4 8.8 %copy-start.3 = (f32[3,4,256,128]{3,2,1,0:T(8,128)}, f32[3,4,256,128]{3,2,1,0:T(8,128)S(1)}, u32[]{:S(2)}) copy-start(f32[3,4,256,128]{3,2,1,0:T(8,128)S(1)} %fusion.17) | copy-start | bytes 4718596
  118.2 33.1 %copy-start.4 = (f32[2,4,8,4,4,256]{5,4,3,2,1,0:T(4,128)}, f32[2,4,8,4,4,256]{5,4,3,2,1,0:T(4,128)S(1)}, u32[]{:S(2)}) copy-start(f32[2,4,8,4,4,256]{5,4,3,2,1,0:T(4,128)S(1)} %multiply_add_fusion) | copy-start | bytes 3145732
